TPU v7x, 32 devices: a whole 2x2x4 slice. The times are simulated.
32 devices in a mesh: dz: 4 (over x, core), dxy: 8 (over z, y).
Axes of the slice: x: 2, y: 2, z: 4, core: 2. Of those that a mesh axis runs over, the one named last changes fastest.
Arguments:
- queries: bfloat16 [4096, 1024], P(('dz', 'dxy')), may hold values from -180 to 180
- keys: bfloat16 [4096, 1024], P(('dz', 'dxy')), may hold values from -4 to 4
- values: bfloat16 [4096, 1024], P(('dz', 'dxy')), may hold values from -6 to 6
- out_grad: bfloat16 [4096, 1024], P(('dz', 'dxy')), may hold values from -6 to 6
- out_weight: bfloat16 [1024, 1024], replicated, may hold values from -0.1875 to 0.1875
- pair_counts: int32 [32, 9], P(('dz', 'dxy')), may hold values from 0 to 128, as said below
- counts: int32 [32], P(('dz', 'dxy')), may hold values from 2 to 128
Outputs:
- gradient_of_queries: bfloat16 [4096, 1024], P(('dz', 'dxy'))
- gradient_of_keys: bfloat16 [4096, 1024], P(('dz', 'dxy'))
- gradient_of_values: bfloat16 [4096, 1024], P(('dz', 'dxy'))
- wo_grad: float32 [1024, 1024], P('dxy')
Inputs may be any that keep to these rules, and one draw needn't show every extreme that they name: `pair_counts`: slot ((i + 1) * 3 + (j + 1)) + t of cell c refers to cell t of the domain at offset (i, j) from c's domain; its entry is that cell's entry of counts when the two cells are linked, else 0, and always 0 where the domain lies outside the grid. Links are symmetric and every cell is linked to itself.
All inputs are finite; a program needn't handle non-finite values.
Results may differ from a plain program's by a relative error of at most 0.02.
Values may be sent and summed in bfloat16 or wider, within the bound.
No kernel may reach another device: no remote copies, remote signals or barrier semaphores. Data moves between devices by JAX's collectives and lax.ppermute only.
A program may use at most 128 MiB of HBM per device.

v0:
```python
import jax
import jax.numpy as jnp
from jax import lax
from jax.sharding import PartitionSpec as P

HEADS = 16
CELL = 128
GROUP_HEADS = 4


def extended(block, sides, width):
    for axis, dim in sides:
        count = lax.axis_size(axis)
        forward = [(i, i + 1) for i in range(count - 1)]
        backward = [(target, source) for source, target in forward]
        low = lax.ppermute(
            lax.slice_in_dim(block, block.shape[dim] - width, None, axis=dim), axis, forward
        )
        high = lax.ppermute(lax.slice_in_dim(block, 0, width, axis=dim), axis, backward)
        block = jnp.concatenate([low, block, high], axis=dim)
    return block


def shifted(value, axis, by):
    count = lax.axis_size(axis)
    pairs = [(i, i + by) for i in range(count) if 0 <= i + by < count]
    return lax.ppermute(value, axis, pairs)


def shards(queries, keys, values, out_grad, out_weight, pair_counts, counts):
    row_count, model_width = queries.shape
    head_width = model_width // HEADS
    logit_scale = head_width ** (-0.5)
    local_cells = counts.shape[0]
    key_rows = pair_counts.shape[1] * CELL
    group_width = GROUP_HEADS * head_width
    atom_index = jnp.arange(CELL, dtype=jnp.int32)
    live_rows = (atom_index[None, :] < counts[:, None]).reshape(row_count, 1)
    masked_grad = jnp.where(live_rows, out_grad, jnp.zeros_like(out_grad))
    out_delta = jnp.dot(masked_grad, out_weight, preferred_element_type=jnp.float32).astype(
        jnp.bfloat16
    )
    stacked = jnp.concatenate([keys, values], axis=1)[None, None]
    surround = extended(stacked, (("dz", 0), ("dxy", 1)), 1)
    surround = surround.reshape(key_rows, 2 * model_width)
    adjacent_keys = surround[:, :model_width]
    adjacent_values = surround[:, model_width:]
    allowed = (atom_index[None, None, :] < pair_counts[:, :, None]).reshape(local_cells, key_rows)
    allowed = jnp.repeat(allowed, CELL, axis=0)[None]
    query_parts, attended_parts, lse_parts, delta_parts, near_key_parts, near_value_parts = (
        [],
        [],
        [],
        [],
        [],
        [],
    )
    for group_id in range(HEADS // GROUP_HEADS):
        columns = slice(group_id * group_width, (group_id + 1) * group_width)
        cluster_queries = queries[:, columns].reshape(row_count, GROUP_HEADS, head_width)
        cluster_delta = out_delta[:, columns].reshape(row_count, GROUP_HEADS, head_width)
        cluster_keys = adjacent_keys[:, columns].reshape(key_rows, GROUP_HEADS, head_width)
        cluster_values = adjacent_values[:, columns].reshape(key_rows, GROUP_HEADS, head_width)
        attention_logits = logit_scale * jnp.einsum(
            "qvy,pvy->vqp", cluster_queries, cluster_keys, preferred_element_type=jnp.float32
        )
        attention_logits = jnp.where(allowed, attention_logits, -1e30)
        highest = jnp.max(attention_logits, axis=-1, keepdims=True)
        weight_sum = jnp.sum(
            jnp.where(allowed, jnp.exp(attention_logits - highest), 0.0), axis=-1, keepdims=True
        )
        log_total = highest + jnp.log(weight_sum)
        probs = jnp.where(allowed, jnp.exp(attention_logits - log_total), 0.0)
        probabilities_reduced = probs.astype(jnp.bfloat16)
        attention_result = jnp.einsum(
            "gtl,lgs->tgs",
            probabilities_reduced,
            cluster_values,
            preferred_element_type=jnp.float32,
        ).astype(jnp.bfloat16)
        row_delta = jnp.sum(
            cluster_delta.astype(jnp.float32) * attention_result.astype(jnp.float32), axis=-1
        )
        probability_gradient = jnp.einsum(
            "qvy,pvy->vqp", cluster_delta, cluster_values, preferred_element_type=jnp.float32
        )
        score_gradient = (probs * (probability_gradient - row_delta.T[:, :, None])).astype(
            jnp.bfloat16
        )
        group_grad = logit_scale * jnp.einsum(
            "gtl,lgs->tgs", score_gradient, cluster_keys, preferred_element_type=jnp.float32
        )
        query_parts.append(group_grad.astype(jnp.bfloat16).reshape(row_count, group_width))
        attended_parts.append(attention_result.reshape(row_count, group_width))
        lse_parts.append(log_total[:, :, 0])
        delta_parts.append(row_delta.T)
        value_part = jnp.einsum(
            "snq,nst->qst", probabilities_reduced, cluster_delta, preferred_element_type=jnp.float32
        )
        key_part = logit_scale * jnp.einsum(
            "snq,nst->qst", score_gradient, cluster_queries, preferred_element_type=jnp.float32
        )
        near_key_parts.append(key_part.reshape(key_rows, group_width))
        near_value_parts.append(value_part.reshape(key_rows, group_width))
    gradient_of_queries = jnp.concatenate(query_parts, axis=1)
    attended_all = jnp.concatenate(attended_parts, axis=1)
    key_partials = jnp.concatenate(near_key_parts + near_value_parts, axis=1).reshape(
        3, 3, row_count, 2 * model_width
    )
    column_sums = key_partials[1]
    for layer_slot, offset in ((0, -1), (2, 1)):
        column_sums = column_sums + shifted(key_partials[layer_slot], "dz", offset)
    owned = column_sums[1]
    for place_slot, offset in ((0, -1), (2, 1)):
        owned = owned + shifted(column_sums[place_slot], "dxy", offset)
    gradient_of_keys = owned[:, :model_width].astype(jnp.bfloat16)
    gradient_of_values = owned[:, model_width:].astype(jnp.bfloat16)
    device_count = lax.axis_size("dz") * lax.axis_size("dxy")
    normalizer = (row_count * device_count) ** (-0.5)
    plane_rows = lax.psum_scatter(
        lax.dot_general(
            masked_grad, attended_all, (((0,), (0,)), ((), ())), preferred_element_type=jnp.float32
        ),
        "dxy",
        scatter_dimension=0,
        tiled=True,
    )
    wo_grad = lax.psum(plane_rows, "dz") * normalizer
    return (gradient_of_queries, gradient_of_keys, gradient_of_values, wo_grad)


def solution(mesh):
    in_specs = (
        P(("dz", "dxy"), None),
        P(("dz", "dxy"), None),
        P(("dz", "dxy"), None),
        P(("dz", "dxy"), None),
        P(),
        P(("dz", "dxy"), None),
        P(("dz", "dxy")),
    )
    out_specs = (
        P(("dz", "dxy"), None),
        P(("dz", "dxy"), None),
        P(("dz", "dxy"), None),
        P("dxy", None),
    )
    return jax.shard_map(shards, mesh=mesh, in_specs=in_specs, out_specs=out_specs, check_vma=False)
```

profile of v0, /device:TPU:0, one launch (start us, length us, event | category | flops | bytes accessed | tf_op | source)
XLA Modules:
  0.0 288.1 jit_solution(11194550064958345261)
XLA Ops:
  7.2 1.2 maximum_bitcast_fusion
  8.5 1.3 collective-permute-start.1
  9.8 3.1 %collective-permute-start = (bf16[1,1,128,2048]{3,2,1,0:T(8,128)(2,1)S(1)}, bf16[1,1,128,2048]{3,2,1,0:T(8,128)(2,1)S(1)}, u32[]{:S(2)}, u32[]{:S(2)}) collective-permute-start(bf16[1,1,128,2048]{3,2,1,0:T(8,128)(2,1)S(1)} %maximum_bitcast_fusion), channel_id=1, source_target_pairs={{0,8},{8,16},{16,24},{1,9},{9,17},{17,25},{2,10},{10,18},{18,26},{... | collective-permute-start | bytes 1572872 | tf_op jit(solution)/shard_map/ppermute | solution.py:16
  12.8 1.5 collective-permute-done
  14.3 1.4 pad_maximum_fusion.1
  15.7 1.3 collective-permute-start.3
  17.0 6.7 %collective-permute-start.2 = (bf16[3,1,128,2048]{3,2,1,0:T(8,128)(2,1)}, bf16[3,1,128,2048]{3,2,1,0:T(8,128)(2,1)}, u32[]{:S(2)}, u32[]{:S(2)}) collective-permute-start(bf16[3,1,128,2048]{3,2,1,0:T(8,128)(2,1)} %pad_maximum_fusion.1), channel_id=1, source_target_pairs={{0,1},{1,2},{2,3},{3,4},{4,5},{5,6},{6,7},{8,9},{9,10},{10,11},{11... | collective-permute-start | bytes 4718600 | tf_op jit(solution)/shard_map/ppermute | solution.py:16
  25.7 0.7 copy.85
  27.9 1.0 fusion.54
  30.3 0.7 copy.63
  31.0 0.7 copy.84
  31.8 19.1 %collective-permute-done.3 = bf16[3,1,128,2048]{3,2,1,0:T(8,128)(2,1)} collective-permute-done((bf16[3,1,128,2048]{3,2,1,0:T(8,128)(2,1)}, bf16[3,1,128,2048]{3,2,1,0:T(8,128)(2,1)}, u32[]{:S(2)}, u32[]{:S(2)}) %collective-permute-start.3) | collective-permute-done | bytes 1572896 | tf_op jit(solution)/shard_map/ppermute | solution.py:19
  50.9 39.3 %collective-permute-done.2 = bf16[3,1,128,2048]{3,2,1,0:T(8,128)(2,1)} collective-permute-done((bf16[3,1,128,2048]{3,2,1,0:T(8,128)(2,1)}, bf16[3,1,128,2048]{3,2,1,0:T(8,128)(2,1)}, u32[]{:S(2)}, u32[]{:S(2)}) %collective-permute-start.2) | collective-permute-done | bytes 1572896 | tf_op jit(solution)/shard_map/ppermute | solution.py:16
  90.2 2.3 pad_maximum_fusion
  92.5 1.4 fusion.51
  94.2 1.4 copy.131
  95.5 1.1 copy.130
  96.6 1.4 copy.129
  98.0 1.1 copy.128
  99.3 1.6 copy.125
  100.9 1.1 copy.132
  102.0 1.6 fusion.56
  103.6 0.8 fusion.57
  104.4 0.8 fusion.58
  105.2 0.8 fusion.55
  106.0 2.3 select_reduce_fusion.3
  108.9 1.7 fusion.47
  110.6 1.0 fusion.12
  112.9 1.0 fusion.13
  113.9 1.6 convolution_multiply_fusion.6
  116.2 1.0 fusion.14
  117.3 1.6 convolution_multiply_fusion.5
  119.5 1.0 fusion.15
  120.5 1.0 copy-done.13
  121.6 1.6 convolution_multiply_fusion.4
  123.2 2.8 fusion.27
  126.1 1.2 copy-done.20
  127.7 0.9 copy-done.22
  129.1 1.3 copy-done.5
  131.1 0.9 copy-done.3
  133.6 3.3 %fusion.50 = (f32[384,2048]{0,1:T(8,128)}, f32[384,2048]{0,1:T(8,128)}, f32[384,2048]{0,1:T(8,128)S(1)}) fusion(f32[1152,2048]{0,1:T(8,128)S(1)} %constant_dynamic-update-slice_fusion), kind=kLoop, calls=%fused_computation.100 | loop fusion | bytes 18874368 | tf_op jit(solution)/shard_map/slice | solution.py:112
  137.0 3.5 %copy.103 = f32[384,2048]{1,0:T(8,128)} copy(f32[384,2048]{0,1:T(8,128)} %get-tuple-element.8) | data formatting | bytes 6291456 | tf_op jit(solution)/shard_map/slice | solution.py:112
  140.5 3.6 %copy.104 = f32[384,2048]{1,0:T(8,128)} copy(f32[384,2048]{0,1:T(8,128)} %get-tuple-element.9) | data formatting | bytes 6291456 | tf_op jit(solution)/shard_map/slice | solution.py:112
  144.1 3.9 %collective-permute-start.5 = (f32[3,128,2048]{2,1,0:T(8,128)}, f32[3,128,2048]{2,1,0:T(8,128)}, u32[]{:S(2)}, u32[]{:S(2)}) collective-permute-start(f32[3,128,2048]{2,1,0:T(8,128)} %bitcast.169), channel_id=1, source_target_pairs={{0,8},{8,16},{16,24},{1,9},{9,17},{17,25},{2,10},{10,18},{18,26},{... | collective-permute-start | bytes 9437192 | tf_op jit(solution)/shard_map/ppermute | solution.py:27
  148.0 1.3 collective-permute-start.4
  149.3 2.3 copy.102
  151.9 4.0 %collective-permute-done.4 = f32[3,128,2048]{2,1,0:T(8,128)} collective-permute-done((f32[3,128,2048]{2,1,0:T(8,128)}, f32[3,128,2048]{2,1,0:T(8,128)}, u32[]{:S(2)}, u32[]{:S(2)}) %collective-permute-start.4) | collective-permute-done | bytes 3145760 | tf_op jit(solution)/shard_map/ppermute | solution.py:27
  155.9 4.7 %add_add_fusion = f32[3,128,2048]{2,1,0:T(8,128)S(1)} fusion(f32[3,128,2048]{2,1,0:T(8,128)} %collective-permute-done.5, f32[3,128,2048]{2,1,0:T(8,128)} %bitcast.151, f32[3,128,2048]{2,1,0:T(8,128)} %collective-permute-done.4), kind=kLoop, calls=%fused_computation.21 | loop fusion | flops 1572864 | bytes 12582912 | tf_op jit(solution)/shard_map/add | solution.py:112
  160.7 1.7 copy-done.6
  162.3 1.5 slice_bitcast_fusion.1
  163.8 1.4 collective-permute-start.6
  165.2 5.9 %collective-permute-start.7 = (f32[128,2048]{1,0:T(8,128)}, f32[128,2048]{1,0:T(8,128)}, u32[]{:S(2)}, u32[]{:S(2)}) collective-permute-start(f32[128,2048]{1,0:T(8,128)} %get-tuple-element.20), channel_id=1, source_target_pairs={{0,1},{1,2},{2,3},{3,4},{4,5},{5,6},{6,7},{8,9},{9,10},{10,11},{11... | collective-permute-start | bytes 3145736 | tf_op jit(solution)/shard_map/ppermute | solution.py:27
  171.2 1.0 fusion.20
  172.1 1.7 copy.90
  173.8 2.1 fusion.21
  175.9 1.0 copy.91
  176.9 1.4 fusion.22
  178.4 1.4 fusion.23
  180.0 0.7 pad_maximum_fusion.2
  180.7 63.3 %reduce-scatter.2.cloned.1.call-done = f32[128,1024]{1,0:T(8,128)} async-done(((f32[1024,1024]{1,0:T(8,128)}), f32[128,1024]{1,0:T(8,128)}) %reduce-scatter.2.cloned.1.call-update) | async-done | bytes 524304 | tf_op jit(solution)/shard_map/reduce_scatter | solution.py:120
  244.0 2.2 fusion.26
  246.2 0.8 fusion.52
  247.0 32.3 %all-reduce.2.cloned.1.call-done = f32[128,1024]{1,0:T(8,128)} async-done(((f32[128,1024]{1,0:T(8,128)}), f32[128,1024]{1,0:T(8,128)}) %all-reduce.2.cloned.1.call-update) | async-done | bytes 524304 | tf_op jit(solution)/shard_map/psum | solution.py:128
  279.4 1.9 broadcast_multiply_fusion
  (124 shorter events, 11.9 us)
Async XLA Ops:
  7.2 17.2 %copy-start = (bf16[1024,1024]{1,0:T(8,128)(2,1)S(1)}, bf16[1024,1024]{1,0:T(8,128)(2,1)}, u32[]{:S(2)}) copy-start(bf16[1024,1024]{1,0:T(8,128)(2,1)} %param.11) | copy-start | bytes 6291460
  7.2 17.2 %copy-start.28 = (bf16[128,1024]{1,0:T(8,128)(2,1)S(1)}, bf16[128,1024]{1,0:T(8,128)(2,1)}, u32[]{:S(2)}) copy-start(bf16[128,1024]{1,0:T(8,128)(2,1)} %param.10) | copy-start | bytes 786436
  7.2 236.8 %reduce-scatter.2.cloned.1.call-start = ((), (), s32[]{:S(2)}) async-start(), calls=%async_computation.1 | async-start | bytes 4718592 | tf_op jit(solution)/shard_map/reduce_scatter | solution.py:120
  8.5 4.4 %collective-permute-start.1 = (bf16[1,1,128,2048]{3,2,1,0:T(8,128)(2,1)S(1)}, bf16[1,1,128,2048]{3,2,1,0:T(8,128)(2,1)S(1)}, u32[]{:S(2)}, u32[]{:S(2)}) collective-permute-start(bf16[1,1,128,2048]{3,2,1,0:T(8,128)(2,1)S(1)} %maximum_bitcast_fusion), channel_id=1, source_target_pairs={{8,0},{16,8},{24,16},{9,1},{17,9},{25,17},{10,2},{18,10},{26,18},{... | collective-permute-start | bytes 1572872 | tf_op jit(solution)/shard_map/ppermute | solution.py:19
  9.8 4.6 %collective-permute-start = (bf16[1,1,128,2048]{3,2,1,0:T(8,128)(2,1)S(1)}, bf16[1,1,128,2048]{3,2,1,0:T(8,128)(2,1)S(1)}, u32[]{:S(2)}, u32[]{:S(2)}) collective-permute-start(bf16[1,1,128,2048]{3,2,1,0:T(8,128)(2,1)S(1)} %maximum_bitcast_fusion), channel_id=1, source_target_pairs={{0,8},{8,16},{16,24},{1,9},{9,17},{17,25},{2,10},{10,18},{18,26},{... | collective-permute-start | bytes 1572872 | tf_op jit(solution)/shard_map/ppermute | solution.py:16
  14.3 10.6 %copy-start.27 = (bf16[1,1,128,2048]{3,2,1,0:T(8,128)(2,1)}, bf16[1,1,128,2048]{3,2,1,0:T(8,128)(2,1)S(1)}, u32[]{:S(2)}) copy-start(bf16[1,1,128,2048]{3,2,1,0:T(8,128)(2,1)S(1)} %collective-permute-done) | copy-start | bytes 1572868
  15.7 35.2 %collective-permute-start.3 = (bf16[3,1,128,2048]{3,2,1,0:T(8,128)(2,1)}, bf16[3,1,128,2048]{3,2,1,0:T(8,128)(2,1)}, u32[]{:S(2)}, u32[]{:S(2)}) collective-permute-start(bf16[3,1,128,2048]{3,2,1,0:T(8,128)(2,1)} %pad_maximum_fusion.1), channel_id=1, source_target_pairs={{1,0},{2,1},{3,2},{4,3},{5,4},{6,5},{7,6},{9,8},{10,9},{11,10},{12... | collective-permute-start | bytes 4718600 | tf_op jit(solution)/shard_map/ppermute | solution.py:19
  17.0 73.2 %collective-permute-start.2 = (bf16[3,1,128,2048]{3,2,1,0:T(8,128)(2,1)}, bf16[3,1,128,2048]{3,2,1,0:T(8,128)(2,1)}, u32[]{:S(2)}, u32[]{:S(2)}) collective-permute-start(bf16[3,1,128,2048]{3,2,1,0:T(8,128)(2,1)} %pad_maximum_fusion.1), channel_id=1, source_target_pairs={{0,1},{1,2},{2,3},{3,4},{4,5},{5,6},{6,7},{8,9},{9,10},{10,11},{11... | collective-permute-start | bytes 4718600 | tf_op jit(solution)/shard_map/ppermute | solution.py:16
  24.4 0.6 copy-start.42
  24.4 7.3 %copy-start.44 = (s32[1,9]{1,0:T(1,128)S(1)}, s32[1,9]{1,0:T(1,128)}, u32[]{:S(2)}) copy-start(s32[1,9]{1,0:T(1,128)} %param.12) | copy-start | bytes 112
  95.5 9.7 %copy-start.15 = (bf16[1152,256]{0,1:T(8,128)(2,1)}, bf16[1152,256]{0,1:T(8,128)(2,1)S(1)}, u32[]{:S(2)}) copy-start(bf16[1152,256]{0,1:T(8,128)(2,1)S(1)} %copy.131) | copy-start | bytes 1769476
  97.9 6.4 %copy-start.16 = (bf16[1152,256]{0,1:T(8,128)(2,1)}, bf16[1152,256]{0,1:T(8,128)(2,1)S(1)}, u32[]{:S(2)}) copy-start(bf16[1152,256]{0,1:T(8,128)(2,1)S(1)} %copy.129) | copy-start | bytes 1769476
  99.3 4.3 %copy-start.17 = (bf16[1152,256]{0,1:T(8,128)(2,1)}, bf16[1152,256]{0,1:T(8,128)(2,1)S(1)}, u32[]{:S(2)}) copy-start(bf16[1152,256]{0,1:T(8,128)(2,1)S(1)} %copy.127) | copy-start | bytes 1769476
  100.9 3.5 %copy-start.18 = (bf16[1152,256]{0,1:T(8,128)(2,1)}, bf16[1152,256]{0,1:T(8,128)(2,1)S(1)}, u32[]{:S(2)}) copy-start(bf16[1152,256]{0,1:T(8,128)(2,1)S(1)} %copy.125) | copy-start | bytes 1769476
  102.0 1.6 copy-start.39
  102.0 2.4 copy-start.38
  103.6 1.6 copy-start.37
  104.4 8.5 %copy-start.4 = (f32[4,128,1152]{1,2,0:T(8,128)}, f32[4,128,1152]{1,2,0:T(8,128)S(1)}, u32[]{:S(2)}) copy-start(f32[4,128,1152]{1,2,0:T(8,128)S(1)} %get-tuple-element.36) | copy-start | bytes 7077892
  105.2 11.0 %copy-start.2 = (f32[4,128,1152]{1,2,0:T(8,128)}, f32[4,128,1152]{1,2,0:T(8,128)S(1)}, u32[]{:S(2)}) copy-start(f32[4,128,1152]{1,2,0:T(8,128)S(1)} %get-tuple-element.38) | copy-start | bytes 7077892
  106.0 2.3 copy-start.36
  110.6 1.0 copy-start.40
  110.6 1.6 copy-start.26
  110.6 1.6 copy-start.34
  111.6 1.3 copy-start.7
  112.9 2.7 copy-start.24
  112.9 2.7 copy-start.32
  113.9 2.3 copy-start.9
  116.2 2.7 copy-start.25
  116.2 2.7 copy-start.30
  117.3 2.3 copy-start.11
  119.5 3.6 %copy-start.29 = (bf16[128,1024]{1,0:T(8,128)(2,1)S(1)}, bf16[128,1024]{1,0:T(8,128)(2,1)}, u32[]{:S(2)}) copy-start(bf16[128,1024]{1,0:T(8,128)(2,1)} %param.10) | copy-start | bytes 786436
  119.5 3.6 %copy-start.43 = (pred[128]{0:T(512)(128)(4,1)S(1)}, pred[128]{0:T(512)(128)(4,1)}, u32[]{:S(2)}) copy-start(pred[128]{0:T(512)(128)(4,1)} %copy-done.42) | copy-start | bytes 388
  120.5 1.0 copy-start.13
  126.0 153.4 %all-reduce.2.cloned.1.call-start = ((), (), s32[]{:S(2)}) async-start(), calls=%async_computation.2 | async-start | bytes 1048576 | tf_op jit(solution)/shard_map/psum | solution.py:128
  126.0 1.3 copy-start.20
  126.0 1.6 copy-start.21
  127.3 1.4 copy-start.22
  127.7 1.3 copy-start.23
  128.7 1.7 copy-start.5
  128.7 1.7 copy-start.35
  130.4 1.7 copy-start.3
  130.4 1.7 copy-start.33
  132.1 0.8 copy-start.31
  144.1 7.8 %collective-permute-start.5 = (f32[3,128,2048]{2,1,0:T(8,128)}, f32[3,128,2048]{2,1,0:T(8,128)}, u32[]{:S(2)}, u32[]{:S(2)}) collective-permute-start(f32[3,128,2048]{2,1,0:T(8,128)} %bitcast.169), channel_id=1, source_target_pairs={{0,8},{8,16},{16,24},{1,9},{9,17},{17,25},{2,10},{10,18},{18,26},{... | collective-permute-start | bytes 9437192 | tf_op jit(solution)/shard_map/ppermute | solution.py:27
  148.0 7.9 %collective-permute-start.4 = (f32[3,128,2048]{2,1,0:T(8,128)}, f32[3,128,2048]{2,1,0:T(8,128)}, u32[]{:S(2)}, u32[]{:S(2)}) collective-permute-start(f32[3,128,2048]{2,1,0:T(8,128)} %bitcast.168), channel_id=1, source_target_pairs={{8,0},{16,8},{24,16},{9,1},{17,9},{25,17},{10,2},{18,10},{26,18},{... | collective-permute-start | bytes 9437192 | tf_op jit(solution)/shard_map/ppermute | solution.py:27
  160.6 1.7 copy-start.6
  162.3 8.8 %copy-start.8 = (bf16[4,128,1152]{1,2,0:T(8,128)(2,1)S(1)}, bf16[4,128,1152]{1,2,0:T(8,128)(2,1)}, u32[]{:S(2)}) copy-start(bf16[4,128,1152]{1,2,0:T(8,128)(2,1)} %copy-done.7) | copy-start | bytes 3538948
  162.3 8.8 %copy-start.19 = (bf16[1152,256]{0,1:T(8,128)(2,1)S(1)}, bf16[1152,256]{0,1:T(8,128)(2,1)}, u32[]{:S(2)}) copy-start(bf16[1152,256]{0,1:T(8,128)(2,1)} %copy-done.18) | copy-start | bytes 1769476
  162.3 11.5 %copy-start.10 = (bf16[4,128,1152]{1,2,0:T(8,128)(2,1)S(1)}, bf16[4,128,1152]{1,2,0:T(8,128)(2,1)}, u32[]{:S(2)}) copy-start(bf16[4,128,1152]{1,2,0:T(8,128)(2,1)} %copy-done.9) | copy-start | bytes 3538948
  163.8 13.1 %copy-start.12 = (bf16[4,128,1152]{1,2,0:T(8,128)(2,1)S(1)}, bf16[4,128,1152]{1,2,0:T(8,128)(2,1)}, u32[]{:S(2)}) copy-start(bf16[4,128,1152]{1,2,0:T(8,128)(2,1)} %copy-done.11) | copy-start | bytes 3538948
  163.8 80.2 %collective-permute-start.6 = (f32[128,2048]{1,0:T(8,128)}, f32[128,2048]{1,0:T(8,128)}, u32[]{:S(2)}, u32[]{:S(2)}) collective-permute-start(f32[128,2048]{1,0:T(8,128)} %get-tuple-element.19), channel_id=1, source_target_pairs={{1,0},{2,1},{3,2},{4,3},{5,4},{6,5},{7,6},{9,8},{10,9},{11,10},{12... | collective-permute-start | bytes 3145736 | tf_op jit(solution)/shard_map/ppermute | solution.py:27
  165.2 78.8 %collective-permute-start.7 = (f32[128,2048]{1,0:T(8,128)}, f32[128,2048]{1,0:T(8,128)}, u32[]{:S(2)}, u32[]{:S(2)}) collective-permute-start(f32[128,2048]{1,0:T(8,128)} %get-tuple-element.20), channel_id=1, source_target_pairs={{0,1},{1,2},{2,3},{3,4},{4,5},{5,6},{6,7},{8,9},{9,10},{10,11},{11... | collective-permute-start | bytes 3145736 | tf_op jit(solution)/shard_map/ppermute | solution.py:27
  172.1 6.3 %copy-start.14 = (bf16[4,128,1152]{1,2,0:T(8,128)(2,1)S(1)}, bf16[4,128,1152]{1,2,0:T(8,128)(2,1)}, u32[]{:S(2)}) copy-start(bf16[4,128,1152]{1,2,0:T(8,128)(2,1)} %copy-done.13) | copy-start | bytes 3538948
  175.9 4.1 %copy-start.41 = (bf16[128,256]{1,0:T(8,128)(2,1)S(1)}, bf16[128,256]{1,0:T(8,128)(2,1)}, u32[]{:S(2)}) copy-start(bf16[128,256]{1,0:T(8,128)(2,1)} %copy.90) | copy-start | bytes 196612
  244.0 37.2 %copy-start.1 = (bf16[1024,1024]{1,0:T(8,128)(2,1)S(1)}, bf16[1024,1024]{1,0:T(8,128)(2,1)}, u32[]{:S(2)}) copy-start(bf16[1024,1024]{1,0:T(8,128)(2,1)} %param.11) | copy-start | bytes 6291460
Sparse Core Ops, SparseCore 0:
  126.1 117.8 reduce-scatter.1
  246.3 32.9 all-reduce.1
where the time goes:
time: 289 us; the launch traced here: 288 us
  waiting for transfers between devices  160 us (55%)
  local copies, waits for them, and re-layouts  42.7 us (15%)
  matrix products  28.6 us (10%)
  starting transfers between devices  25 us (9%)
  other arithmetic  16.7 us (6%)
  between operations  15.4 us (5%)
    reduce_scatter x1, waiting for transfers between devices, shards(): lax.psum_scatter(lax.dot_general(masked_grad, attended_all, (((0,), (0,))...  63.3 us
    ppermute x2, waiting for transfers between devices, extended(): lax.ppermute(lax.slice_in_dim(block, block.shape[dim] - width, None, axis...  40.7 us
    psum x1, waiting for transfers between devices, shards(): wo_grad = lax.psum(plane_rows, 'dz') * normalizer  32.3 us
    ppermute x2, waiting for transfers between devices, extended(): lax.ppermute(lax.slice_in_dim(block, 0, width, axis=dim), axis, backward)  19.1 us
    unnamed x105, local copies, waits for them, and re-layouts  16.4 us
    ppermute x4, starting transfers between devices, shifted(): return lax.ppermute(value, axis, pairs)  12.5 us
    slice x3, local copies, waits for them, and re-layouts, shards(): column_sums = column_sums + shifted(key_partials[layer_slot], 'dz', offset)  10.5 us
    ppermute x2, starting transfers between devices, extended(): lax.ppermute(lax.slice_in_dim(block, block.shape[dim] - width, None, axis...  9.78 us
  transfers between devices with their start and end apart: 10, of which 7 were waited for; matrix products, arithmetic and copies ran while one was open for 14% of the time, Pallas kernels for 0%

commit v1 on v0

--- a/solution.py
+++ b/solution.py
@@ -2,6 +2,7 @@
 import jax.numpy as jnp
 from jax import lax
 from jax.sharding import PartitionSpec as P
+from jax.lax import all_gather
 
 HEADS = 16
 CELL = 128
@@ -125,7 +126,7 @@
         scatter_dimension=0,
         tiled=True,
     )
-    wo_grad = lax.psum(plane_rows, "dz") * normalizer
+    wo_grad = all_gather(plane_rows, axis_name="dz").sum(axis=0) * normalizer
     return (gradient_of_queries, gradient_of_keys, gradient_of_values, wo_grad)
 
 

time: 289 us -> 279 us (0.965)
  waiting for transfers between devices: 160 us -> 152 us
    psum x1 -> x0, waiting for transfers between devices: 32.3 us -> none  [shards(): wo_grad = lax.psum(plane_rows, 'dz') * normalizer]
    ppermute x4, waiting for transfers between devices: 4.26 us -> 32.6 us  [shifted(): return lax.ppermute(value, axis, pairs)]
    reduce_scatter x1, waiting for transfers between devices: 63.3 us -> 59.6 us  [shards(): lax.psum_scatter(lax.dot_general(masked_grad, attended_all, (((0,), (0,))...]
    unnamed x105 -> x121, local copies, waits for them, and re-layouts: 16.4 us -> 15.6 us
  transfers between devices with their start and end apart: 10 -> 10, of which waited for: 7 -> 6; matrix products, arithmetic and copies ran while one was open for 14% -> 16% of each run, Pallas kernels for 0% -> 0%
where the time goes in v1:
time: 279 us; the launch traced here: 278 us
  waiting for transfers between devices  152 us (54%)
  local copies, waits for them, and re-layouts  41.9 us (15%)
  matrix products  26.6 us (10%)
  starting transfers between devices  24.6 us (9%)
  other arithmetic  17.4 us (6%)
  between operations  15.5 us (6%)
    reduce_scatter x1, waiting for transfers between devices, shards(): lax.psum_scatter(lax.dot_general(masked_grad, attended_all, (((0,), (0,))...  59.6 us
    ppermute x2, waiting for transfers between devices, extended(): lax.ppermute(lax.slice_in_dim(block, block.shape[dim] - width, None, axis...  40.7 us
    ppermute x4, waiting for transfers between devices, shifted(): return lax.ppermute(value, axis, pairs)  32.6 us
    ppermute x2, waiting for transfers between devices, extended(): lax.ppermute(lax.slice_in_dim(block, 0, width, axis=dim), axis, backward)  19.1 us
    unnamed x121, local copies, waits for them, and re-layouts  15.6 us
    ppermute x4, starting transfers between devices, shifted(): return lax.ppermute(value, axis, pairs)  12.2 us
    slice x3, local copies, waits for them, and re-layouts, shards(): column_sums = column_sums + shifted(key_partials[layer_slot], 'dz', offset)  10.4 us
    ppermute x2, starting transfers between devices, extended(): lax.ppermute(lax.slice_in_dim(block, block.shape[dim] - width, None, axis...  9.77 us
  transfers between devices with their start and end apart: 10, of which 6 were waited for; matrix products, arithmetic and copies ran while one was open for 16% of the time, Pallas kernels for 0%

profile of v1, /device:TPU:0, one launch (start us, length us, event | category | flops | bytes accessed | tf_op | source)
XLA Modules:
  0.0 278.1 jit_solution(3389136567641179599)
XLA Ops:
  7.2 1.2 maximum_bitcast_fusion
  8.5 1.3 collective-permute-start.1
  9.8 3.1 %collective-permute-start = (bf16[1,1,128,2048]{3,2,1,0:T(8,128)(2,1)S(1)}, bf16[1,1,128,2048]{3,2,1,0:T(8,128)(2,1)S(1)}, u32[]{:S(2)}, u32[]{:S(2)}) collective-permute-start(bf16[1,1,128,2048]{3,2,1,0:T(8,128)(2,1)S(1)} %maximum_bitcast_fusion), channel_id=1, source_target_pairs={{0,8},{8,16},{16,24},{1,9},{9,17},{17,25},{2,10},{10,18},{18,26},{... | collective-permute-start | bytes 1572872 | tf_op jit(solution)/shard_map/ppermute | solution.py:17
  12.8 1.5 collective-permute-done
  14.3 1.4 pad_maximum_fusion.1
  15.7 1.3 collective-permute-start.3
  17.0 6.7 %collective-permute-start.2 = (bf16[3,1,128,2048]{3,2,1,0:T(8,128)(2,1)}, bf16[3,1,128,2048]{3,2,1,0:T(8,128)(2,1)}, u32[]{:S(2)}, u32[]{:S(2)}) collective-permute-start(bf16[3,1,128,2048]{3,2,1,0:T(8,128)(2,1)} %pad_maximum_fusion.1), channel_id=1, source_target_pairs={{0,1},{1,2},{2,3},{3,4},{4,5},{5,6},{6,7},{8,9},{9,10},{10,11},{11... | collective-permute-start | bytes 4718600 | tf_op jit(solution)/shard_map/ppermute | solution.py:17
  25.7 0.7 copy.85
  27.8 1.0 fusion.54
  28.8 0.7 copy.77
  29.5 0.7 copy.70
  30.2 0.7 copy.63
  31.0 0.7 copy.84
  31.8 19.1 %collective-permute-done.3 = bf16[3,1,128,2048]{3,2,1,0:T(8,128)(2,1)} collective-permute-done((bf16[3,1,128,2048]{3,2,1,0:T(8,128)(2,1)}, bf16[3,1,128,2048]{3,2,1,0:T(8,128)(2,1)}, u32[]{:S(2)}, u32[]{:S(2)}) %collective-permute-start.3) | collective-permute-done | bytes 1572896 | tf_op jit(solution)/shard_map/ppermute | solution.py:20
  50.9 39.3 %collective-permute-done.2 = bf16[3,1,128,2048]{3,2,1,0:T(8,128)(2,1)} collective-permute-done((bf16[3,1,128,2048]{3,2,1,0:T(8,128)(2,1)}, bf16[3,1,128,2048]{3,2,1,0:T(8,128)(2,1)}, u32[]{:S(2)}, u32[]{:S(2)}) %collective-permute-start.2) | collective-permute-done | bytes 1572896 | tf_op jit(solution)/shard_map/ppermute | solution.py:17
  90.2 2.3 pad_maximum_fusion
  92.5 1.4 fusion.51
  94.1 1.4 copy.131
  95.5 1.1 copy.130
  96.6 1.4 copy.129
  97.9 1.1 copy.128
  99.3 1.6 copy.125
  100.9 1.1 copy.132
  101.9 1.6 fusion.56
  103.6 0.8 fusion.57
  104.4 0.8 fusion.58
  105.2 0.8 fusion.55
  105.9 2.3 select_reduce_fusion.3
  108.9 1.0 fusion.12
  111.2 1.0 fusion.13
  112.3 1.6 convolution_multiply_fusion.6
  113.9 1.2 multiply_reduce_fusion
  115.1 1.2 multiply_reduce_fusion.1
  116.4 2.8 %fusion.27 = f32[1024,1024]{1,0:T(8,128)} fusion(bf16[128,256]{0,1:T(8,128)(2,1)S(1)} %bitcast.202, bf16[128,256]{0,1:T(8,128)(2,1)S(1)} %bitcast.203, bf16[128,256]{0,1:T(8,128)(2,1)S(1)} %bitcast.201, bf16[128,256]{0,1:T(8,128)(2,1)S(1)} %bitcast.200, bf16[128,1024]{1,0:T(8,128)(2,1)S(1)} %copy-done.30, pred[128]{0:T(512)(128)(4,1)S(1)} %copy-done.51), kind=kOutput, calls=%fused_computation.64 | convolution fusion | flops 269615104 | bytes 4718720 | tf_op jit(solution)/shard_map/dot_general | solution.py:122
  119.4 1.1 copy-done.22
  121.4 1.0 fusion.14
  123.9 1.0 fusion.15
  126.0 1.0 copy-done.7
  127.7 1.0 copy-done.5
  130.9 3.3 %fusion.50 = (f32[384,2048]{0,1:T(8,128)}, f32[384,2048]{0,1:T(8,128)}, f32[384,2048]{0,1:T(8,128)S(1)}) fusion(f32[1152,2048]{0,1:T(8,128)S(1)} %constant_dynamic-update-slice_fusion), kind=kLoop, calls=%fused_computation.100 | loop fusion | bytes 18874368 | tf_op jit(solution)/shard_map/slice | solution.py:113
  134.2 3.6 %copy.103 = f32[384,2048]{1,0:T(8,128)} copy(f32[384,2048]{0,1:T(8,128)} %get-tuple-element.8) | data formatting | bytes 6291456 | tf_op jit(solution)/shard_map/slice | solution.py:113
  137.7 3.6 %copy.104 = f32[384,2048]{1,0:T(8,128)} copy(f32[384,2048]{0,1:T(8,128)} %get-tuple-element.9) | data formatting | bytes 6291456 | tf_op jit(solution)/shard_map/slice | solution.py:113
  141.3 3.8 %collective-permute-start.5 = (f32[3,128,2048]{2,1,0:T(8,128)}, f32[3,128,2048]{2,1,0:T(8,128)}, u32[]{:S(2)}, u32[]{:S(2)}) collective-permute-start(f32[3,128,2048]{2,1,0:T(8,128)} %bitcast.170), channel_id=1, source_target_pairs={{0,8},{8,16},{16,24},{1,9},{9,17},{17,25},{2,10},{10,18},{18,26},{... | collective-permute-start | bytes 9437192 | tf_op jit(solution)/shard_map/ppermute | solution.py:28
  145.1 1.3 collective-permute-start.4
  146.4 2.4 copy.102
  148.8 59.6 %reduce-scatter.2.cloned.1.call-done = f32[128,1024]{1,0:T(8,128)} async-done(((f32[1024,1024]{1,0:T(8,128)}), f32[128,1024]{1,0:T(8,128)}) %reduce-scatter.2.cloned.1.call-update) | async-done | bytes 524304 | tf_op jit(solution)/shard_map/reduce_scatter | solution.py:121
  208.4 4.7 %add_add_fusion = f32[3,128,2048]{2,1,0:T(8,128)S(1)} fusion(f32[3,128,2048]{2,1,0:T(8,128)} %collective-permute-done.5, f32[3,128,2048]{2,1,0:T(8,128)} %bitcast.152, f32[3,128,2048]{2,1,0:T(8,128)} %collective-permute-done.4), kind=kLoop, calls=%fused_computation.21 | loop fusion | flops 1572864 | bytes 12582912 | tf_op jit(solution)/shard_map/add | solution.py:113
  213.1 1.7 copy-done.8
  214.9 1.5 slice_bitcast_fusion.1
  216.3 1.5 collective-permute-start.6
  217.9 5.5 %collective-permute-start.7 = (f32[128,2048]{1,0:T(8,128)}, f32[128,2048]{1,0:T(8,128)}, u32[]{:S(2)}, u32[]{:S(2)}) collective-permute-start(f32[128,2048]{1,0:T(8,128)} %get-tuple-element.20), channel_id=1, source_target_pairs={{0,1},{1,2},{2,3},{3,4},{4,5},{5,6},{6,7},{8,9},{9,10},{10,11},{11... | collective-permute-start | bytes 3145736 | tf_op jit(solution)/shard_map/ppermute | solution.py:28
  223.4 1.0 fusion.20
  224.4 1.7 copy.90
  226.1 2.1 fusion.21
  228.1 1.0 copy.91
  229.1 1.4 fusion.22
  230.7 1.4 fusion.23
  232.2 0.7 pad_maximum_fusion.2
  233.0 10.2 %collective-permute-done.6 = f32[128,2048]{1,0:T(8,128)} collective-permute-done((f32[128,2048]{1,0:T(8,128)}, f32[128,2048]{1,0:T(8,128)}, u32[]{:S(2)}, u32[]{:S(2)}) %collective-permute-start.6) | collective-permute-done | bytes 1048608 | tf_op jit(solution)/shard_map/ppermute | solution.py:28
  243.2 22.4 %collective-permute-done.7 = f32[128,2048]{1,0:T(8,128)} collective-permute-done((f32[128,2048]{1,0:T(8,128)}, f32[128,2048]{1,0:T(8,128)}, u32[]{:S(2)}, u32[]{:S(2)}) %collective-permute-start.7) | collective-permute-done | bytes 1048608 | tf_op jit(solution)/shard_map/ppermute | solution.py:28
  265.6 2.2 fusion.26
  267.7 0.8 fusion.52
  268.6 1.8 reduce_sum.89
  270.4 0.8 broadcast_multiply_fusion
  (141 shorter events, 12.1 us)
Async XLA Ops:
  7.2 17.2 %copy-start = (bf16[1024,1024]{1,0:T(8,128)(2,1)S(1)}, bf16[1024,1024]{1,0:T(8,128)(2,1)}, u32[]{:S(2)}) copy-start(bf16[1024,1024]{1,0:T(8,128)(2,1)} %param.11) | copy-start | bytes 6291460
  7.2 17.2 %copy-start.29 = (bf16[128,1024]{1,0:T(8,128)(2,1)S(1)}, bf16[128,1024]{1,0:T(8,128)(2,1)}, u32[]{:S(2)}) copy-start(bf16[128,1024]{1,0:T(8,128)(2,1)} %param.10) | copy-start | bytes 786436
  7.2 201.2 %reduce-scatter.2.cloned.1.call-start = ((), (), s32[]{:S(2)}) async-start(), calls=%async_computation.1 | async-start | bytes 4718592 | tf_op jit(solution)/shard_map/reduce_scatter | solution.py:121
  8.5 4.4 %collective-permute-start.1 = (bf16[1,1,128,2048]{3,2,1,0:T(8,128)(2,1)S(1)}, bf16[1,1,128,2048]{3,2,1,0:T(8,128)(2,1)S(1)}, u32[]{:S(2)}, u32[]{:S(2)}) collective-permute-start(bf16[1,1,128,2048]{3,2,1,0:T(8,128)(2,1)S(1)} %maximum_bitcast_fusion), channel_id=1, source_target_pairs={{8,0},{16,8},{24,16},{9,1},{17,9},{25,17},{10,2},{18,10},{26,18},{... | collective-permute-start | bytes 1572872 | tf_op jit(solution)/shard_map/ppermute | solution.py:20
  9.8 4.6 %collective-permute-start = (bf16[1,1,128,2048]{3,2,1,0:T(8,128)(2,1)S(1)}, bf16[1,1,128,2048]{3,2,1,0:T(8,128)(2,1)S(1)}, u32[]{:S(2)}, u32[]{:S(2)}) collective-permute-start(bf16[1,1,128,2048]{3,2,1,0:T(8,128)(2,1)S(1)} %maximum_bitcast_fusion), channel_id=1, source_target_pairs={{0,8},{8,16},{16,24},{1,9},{9,17},{17,25},{2,10},{10,18},{18,26},{... | collective-permute-start | bytes 1572872 | tf_op jit(solution)/shard_map/ppermute | solution.py:17
  14.3 10.6 %copy-start.28 = (bf16[1,1,128,2048]{3,2,1,0:T(8,128)(2,1)}, bf16[1,1,128,2048]{3,2,1,0:T(8,128)(2,1)S(1)}, u32[]{:S(2)}) copy-start(bf16[1,1,128,2048]{3,2,1,0:T(8,128)(2,1)S(1)} %collective-permute-done) | copy-start | bytes 1572868
  15.7 35.2 %collective-permute-start.3 = (bf16[3,1,128,2048]{3,2,1,0:T(8,128)(2,1)}, bf16[3,1,128,2048]{3,2,1,0:T(8,128)(2,1)}, u32[]{:S(2)}, u32[]{:S(2)}) collective-permute-start(bf16[3,1,128,2048]{3,2,1,0:T(8,128)(2,1)} %pad_maximum_fusion.1), channel_id=1, source_target_pairs={{1,0},{2,1},{3,2},{4,3},{5,4},{6,5},{7,6},{9,8},{10,9},{11,10},{12... | collective-permute-start | bytes 4718600 | tf_op jit(solution)/shard_map/ppermute | solution.py:20
  17.0 73.2 %collective-permute-start.2 = (bf16[3,1,128,2048]{3,2,1,0:T(8,128)(2,1)}, bf16[3,1,128,2048]{3,2,1,0:T(8,128)(2,1)}, u32[]{:S(2)}, u32[]{:S(2)}) collective-permute-start(bf16[3,1,128,2048]{3,2,1,0:T(8,128)(2,1)} %pad_maximum_fusion.1), channel_id=1, source_target_pairs={{0,1},{1,2},{2,3},{3,4},{4,5},{5,6},{6,7},{8,9},{9,10},{10,11},{11... | collective-permute-start | bytes 4718600 | tf_op jit(solution)/shard_map/ppermute | solution.py:17
  24.4 0.6 copy-start.50
  24.4 7.4 %copy-start.52 = (s32[1,9]{1,0:T(1,128)S(1)}, s32[1,9]{1,0:T(1,128)}, u32[]{:S(2)}) copy-start(s32[1,9]{1,0:T(1,128)} %param.12) | copy-start | bytes 112
  95.5 9.7 %copy-start.17 = (bf16[1152,256]{0,1:T(8,128)(2,1)}, bf16[1152,256]{0,1:T(8,128)(2,1)S(1)}, u32[]{:S(2)}) copy-start(bf16[1152,256]{0,1:T(8,128)(2,1)S(1)} %copy.131) | copy-start | bytes 1769476
  97.9 6.4 %copy-start.18 = (bf16[1152,256]{0,1:T(8,128)(2,1)}, bf16[1152,256]{0,1:T(8,128)(2,1)S(1)}, u32[]{:S(2)}) copy-start(bf16[1152,256]{0,1:T(8,128)(2,1)S(1)} %copy.129) | copy-start | bytes 1769476
  99.3 4.3 %copy-start.19 = (bf16[1152,256]{0,1:T(8,128)(2,1)}, bf16[1152,256]{0,1:T(8,128)(2,1)S(1)}, u32[]{:S(2)}) copy-start(bf16[1152,256]{0,1:T(8,128)(2,1)S(1)} %copy.127) | copy-start | bytes 1769476
  100.9 3.5 %copy-start.20 = (bf16[1152,256]{0,1:T(8,128)(2,1)}, bf16[1152,256]{0,1:T(8,128)(2,1)S(1)}, u32[]{:S(2)}) copy-start(bf16[1152,256]{0,1:T(8,128)(2,1)S(1)} %copy.125) | copy-start | bytes 1769476
  101.9 1.6 copy-start.43
  101.9 2.5 copy-start.41
  103.6 5.3 %copy-start.6 = (f32[4,128,1152]{1,2,0:T(8,128)}, f32[4,128,1152]{1,2,0:T(8,128)S(1)}, u32[]{:S(2)}) copy-start(f32[4,128,1152]{1,2,0:T(8,128)S(1)} %get-tuple-element.34) | copy-start | bytes 7077892
  103.6 1.6 copy-start.39
  104.4 6.9 %copy-start.4 = (f32[4,128,1152]{1,2,0:T(8,128)}, f32[4,128,1152]{1,2,0:T(8,128)S(1)}, u32[]{:S(2)}) copy-start(f32[4,128,1152]{1,2,0:T(8,128)S(1)} %get-tuple-element.36) | copy-start | bytes 7077892
  105.1 10.0 %copy-start.2 = (f32[4,128,1152]{1,2,0:T(8,128)}, f32[4,128,1152]{1,2,0:T(8,128)S(1)}, u32[]{:S(2)}) copy-start(f32[4,128,1152]{1,2,0:T(8,128)S(1)} %get-tuple-element.38) | copy-start | bytes 7077892
  105.9 2.3 copy-start.35
  108.9 1.1 copy-start.44
  108.9 1.6 copy-start.27
  108.9 1.6 copy-start.37
  110.0 1.3 copy-start.9
  111.2 2.6 copy-start.25
  111.2 2.6 copy-start.31
  112.3 2.8 %copy-start.11 = (bf16[4,128,1152]{1,2,0:T(8,128)(2,1)}, bf16[4,128,1152]{1,2,0:T(8,128)(2,1)S(1)}, u32[]{:S(2)}) copy-start(bf16[4,128,1152]{1,2,0:T(8,128)(2,1)S(1)} %fusion.13) | copy-start | bytes 3538948
  112.3 2.8 %copy-start.23 = (bf16[1152,256]{0,1:T(8,128)(2,1)S(1)}, bf16[1152,256]{0,1:T(8,128)(2,1)}, u32[]{:S(2)}) copy-start(bf16[1152,256]{0,1:T(8,128)(2,1)} %copy.130) | copy-start | bytes 1769476
  112.3 2.8 %copy-start.33 = (bf16[128,256]{0,1:T(8,128)(2,1)S(1)}, bf16[128,256]{0,1:T(8,128)(2,1)}, u32[]{:S(2)}) copy-start(bf16[128,256]{0,1:T(8,128)(2,1)} %copy.78) | copy-start | bytes 196612
  113.9 2.5 copy-start.46
  115.1 1.3 copy-start.30
  115.1 1.3 copy-start.51
  119.2 149.4 %all-gather.3.cloned.1.call-start = ((), (), s32[]{:S(2)}) async-start(), calls=%async_computation.2 | async-start | bytes 2621440 | tf_op jit(solution)/shard_map/all_gather | solution.py:129
  119.2 1.3 copy-start.22
  119.2 2.0 copy-start.3
  119.2 2.1 copy-start.24
  119.2 2.1 copy-start.34
  119.3 2.1 copy-start.47
  119.3 2.1 copy-start.49
  120.6 1.8 copy-start.42
  122.4 1.0 copy-start.13
  122.4 1.5 copy-start.26
  122.4 1.5 copy-start.32
  122.4 1.5 copy-start.48
  123.4 1.5 copy-start.40
  124.9 1.0 copy-start.15
  124.9 2.1 copy-start.7
  124.9 2.1 copy-start.36
  127.0 1.7 copy-start.5
  127.0 1.7 copy-start.38
  141.3 67.1 %collective-permute-start.5 = (f32[3,128,2048]{2,1,0:T(8,128)}, f32[3,128,2048]{2,1,0:T(8,128)}, u32[]{:S(2)}, u32[]{:S(2)}) collective-permute-start(f32[3,128,2048]{2,1,0:T(8,128)} %bitcast.170), channel_id=1, source_target_pairs={{0,8},{8,16},{16,24},{1,9},{9,17},{17,25},{2,10},{10,18},{18,26},{... | collective-permute-start | bytes 9437192 | tf_op jit(solution)/shard_map/ppermute | solution.py:28
  145.1 63.3 %collective-permute-start.4 = (f32[3,128,2048]{2,1,0:T(8,128)}, f32[3,128,2048]{2,1,0:T(8,128)}, u32[]{:S(2)}, u32[]{:S(2)}) collective-permute-start(f32[3,128,2048]{2,1,0:T(8,128)} %bitcast.169), channel_id=1, source_target_pairs={{8,0},{16,8},{24,16},{9,1},{17,9},{25,17},{10,2},{18,10},{26,18},{... | collective-permute-start | bytes 9437192 | tf_op jit(solution)/shard_map/ppermute | solution.py:28
  213.1 1.8 copy-start.8
  214.9 8.6 %copy-start.10 = (bf16[4,128,1152]{1,2,0:T(8,128)(2,1)S(1)}, bf16[4,128,1152]{1,2,0:T(8,128)(2,1)}, u32[]{:S(2)}) copy-start(bf16[4,128,1152]{1,2,0:T(8,128)(2,1)} %copy-done.9) | copy-start | bytes 3538948
  214.9 8.6 %copy-start.21 = (bf16[1152,256]{0,1:T(8,128)(2,1)S(1)}, bf16[1152,256]{0,1:T(8,128)(2,1)}, u32[]{:S(2)}) copy-start(bf16[1152,256]{0,1:T(8,128)(2,1)} %copy-done.20) | copy-start | bytes 1769476
  214.9 11.2 %copy-start.12 = (bf16[4,128,1152]{1,2,0:T(8,128)(2,1)S(1)}, bf16[4,128,1152]{1,2,0:T(8,128)(2,1)}, u32[]{:S(2)}) copy-start(bf16[4,128,1152]{1,2,0:T(8,128)(2,1)} %copy-done.11) | copy-start | bytes 3538948
  216.3 12.8 %copy-start.14 = (bf16[4,128,1152]{1,2,0:T(8,128)(2,1)S(1)}, bf16[4,128,1152]{1,2,0:T(8,128)(2,1)}, u32[]{:S(2)}) copy-start(bf16[4,128,1152]{1,2,0:T(8,128)(2,1)} %copy-done.13) | copy-start | bytes 3538948
  216.3 26.9 %collective-permute-start.6 = (f32[128,2048]{1,0:T(8,128)}, f32[128,2048]{1,0:T(8,128)}, u32[]{:S(2)}, u32[]{:S(2)}) collective-permute-start(f32[128,2048]{1,0:T(8,128)} %get-tuple-element.19), channel_id=1, source_target_pairs={{1,0},{2,1},{3,2},{4,3},{5,4},{6,5},{7,6},{9,8},{10,9},{11,10},{12... | collective-permute-start | bytes 3145736 | tf_op jit(solution)/shard_map/ppermute | solution.py:28
  217.9 47.7 %collective-permute-start.7 = (f32[128,2048]{1,0:T(8,128)}, f32[128,2048]{1,0:T(8,128)}, u32[]{:S(2)}, u32[]{:S(2)}) collective-permute-start(f32[128,2048]{1,0:T(8,128)} %get-tuple-element.20), channel_id=1, source_target_pairs={{0,1},{1,2},{2,3},{3,4},{4,5},{5,6},{6,7},{8,9},{9,10},{10,11},{11... | collective-permute-start | bytes 3145736 | tf_op jit(solution)/shard_map/ppermute | solution.py:28
  224.4 6.3 %copy-start.16 = (bf16[4,128,1152]{1,2,0:T(8,128)(2,1)S(1)}, bf16[4,128,1152]{1,2,0:T(8,128)(2,1)}, u32[]{:S(2)}) copy-start(bf16[4,128,1152]{1,2,0:T(8,128)(2,1)} %copy-done.15) | copy-start | bytes 3538948
  228.1 4.1 %copy-start.45 = (bf16[128,256]{1,0:T(8,128)(2,1)S(1)}, bf16[128,256]{1,0:T(8,128)(2,1)}, u32[]{:S(2)}) copy-start(bf16[128,256]{1,0:T(8,128)(2,1)} %copy.90) | copy-start | bytes 196612
  265.6 5.7 %copy-start.1 = (bf16[1024,1024]{1,0:T(8,128)(2,1)S(1)}, bf16[1024,1024]{1,0:T(8,128)(2,1)}, u32[]{:S(2)}) copy-start(bf16[1024,1024]{1,0:T(8,128)(2,1)} %param.11) | copy-start | bytes 6291460
Sparse Core Ops, SparseCore 0:
  119.3 89.0 reduce-scatter.1
  209.9 22.1 all-gather.2
